TPU v7x, 256 devices: a whole 4x4x8 slice. The times are simulated.
256 devices in a mesh: tm: 32 (over z, x), fsdp: 8 (over y, core).
Axes of the slice: x: 4, y: 4, z: 8, core: 2. Of those that a mesh axis runs over, the one named last changes fastest.
Arguments:
- frames: bfloat16 [64, 64, 256, 128], P('tm', None, 'fsdp'), may hold values from -6 to 6
- conv_weight: bfloat16 [3, 3, 3, 128, 128], P(None, None, None, None, 'fsdp'), may hold values from -0.109375 to 0.109375
- mix_weight: bfloat16 [3, 128, 128], P(None, None, 'fsdp'), may hold values from -0.3125 to 0.3125
- cotangent: bfloat16 [32, 64, 256, 128], P(None, 'tm', 'fsdp'), may hold values from -0.008239746 to 0.008239746
Outputs:
- encoded: bfloat16 [32, 64, 256, 128], P(None, 'tm', 'fsdp')
- mix_grad: float32 [49152], P(('tm', 'fsdp'))
All inputs are finite; a program needn't handle non-finite values.
Results may differ from a plain program's by a relative error of at most 0.0058.
Values may be sent and summed in bfloat16 or wider, within the bound.
A program may use at most 64 MiB of HBM per device.

v0:
```python
import jax
import jax.numpy as jnp
from jax import lax
from jax.sharding import PartitionSpec as P


def from_behind(block, axis, distance):
    devices = range(lax.axis_size(axis))
    route = [(i - distance, i) for i in devices if i - distance in devices]
    return lax.ppermute(block, axis, route)


def with_halo(cells, sides, width):
    for axis, dim in sides:
        count = lax.axis_size(axis)
        ends = count - 1
        head = lax.slice_in_dim(cells, 0, width, axis=dim)
        tail = lax.slice_in_dim(cells, cells.shape[dim] - width, cells.shape[dim], axis=dim)
        cells = jnp.concatenate(
            [
                lax.ppermute(tail, axis, [(i, (i + 1) % count) for i in range(ends)]),
                cells,
                lax.ppermute(head, axis, [((i + 1) % count, i) for i in range(ends)]),
            ],
            axis=dim,
        )
    return cells


def pool_pairs(hidden):
    shaped = hidden.reshape((hidden.shape[0] // 2, 2) + hidden.shape[1:]).astype(jnp.float32)
    return ((shaped[:, 0] + shaped[:, 1]) * 0.5).astype(jnp.bfloat16)


def delayed(block, offset):
    return jnp.pad(block, ((offset, 0), (0, 0), (0, 0), (0, 0)))[: block.shape[0]]


def local(frames, conv_weight, mix_weight, cotangent):
    full_conv, full_mix = (
        lax.all_gather(conv_weight, "fsdp", axis=4, tiled=True),
        lax.all_gather(mix_weight, "fsdp", axis=2, tiled=True),
    )
    count_frames, height, width, channels = frames.shape
    previous = from_behind(frames, "tm", 1)
    timed = jnp.concatenate([previous, frames], axis=0)
    padded = with_halo(timed, (("fsdp", 2),), 1)
    padded = jnp.pad(padded, ((0, 0), (1, 1), (0, 0), (0, 0)))
    accum = jnp.zeros((count_frames * height * width, channels), jnp.float32)
    for row_tap in range(3):
        for col_tap in range(3):
            stacked = jnp.concatenate(
                [
                    padded[
                        step : step + count_frames,
                        row_tap : row_tap + height,
                        col_tap : col_tap + width,
                        :,
                    ]
                    for step in range(3)
                ],
                axis=3,
            ).reshape(-1, 3 * channels)
            kernel = full_conv[:, row_tap, col_tap].reshape(3 * channels, channels)
            accum = accum + jnp.dot(stacked, kernel, preferred_element_type=jnp.float32)
    hidden = jax.nn.silu(accum).astype(jnp.bfloat16).reshape(count_frames, height, width, channels)
    pooled = lax.all_to_all(pool_pairs(hidden), "tm", split_axis=1, concat_axis=0, tiled=True)
    branch = pooled.astype(jnp.float32).reshape(-1, channels)
    flat_cot = cotangent.reshape(-1, channels)
    grad_terms = []
    for offset in range(3):
        lagged = delayed(pooled, offset).reshape(-1, channels)
        branch = branch + jnp.dot(lagged, full_mix[offset], preferred_element_type=jnp.float32)
        grad_terms.append(
            lax.dot_general(
                lagged, flat_cot, (((0,), (0,)), ((), ())), preferred_element_type=jnp.float32
            )
        )
    encoded = branch.astype(jnp.bfloat16).reshape(pooled.shape)
    parts = lax.axis_size("tm") * lax.axis_size("fsdp")
    mix_grad = lax.all_to_all(
        jnp.stack(grad_terms).reshape(parts, -1), ("tm", "fsdp"), 0, 0, tiled=True
    ).sum(0)
    return (encoded, mix_grad)


def solution(mesh):
    return jax.shard_map(
        local,
        mesh=mesh,
        in_specs=(
            P("tm", None, "fsdp", None),
            P(None, None, None, None, "fsdp"),
            P(None, None, "fsdp"),
            P(None, "tm", "fsdp", None),
        ),
        out_specs=(P(None, "tm", "fsdp", None), P(("tm", "fsdp"))),
        check_vma=False,
    )
```

profile of v0, /device:TPU:1, one launch (start us, length us, event | category | flops | bytes accessed | tf_op | source)
XLA Modules:
  0.0 129.5 jit_solution(5271844698895392121)
XLA Ops:
  0.7 4.1 %collective-permute-start = (bf16[2,64,32,128]{3,2,1,0:T(8,128)(2,1)}, bf16[2,64,32,128]{3,2,1,0:T(8,128)(2,1)S(1)}, u32[]{:S(2)}, u32[]{:S(2)}) collective-permute-start(bf16[2,64,32,128]{3,2,1,0:T(8,128)(2,1)} %param.4), channel_id=1, source_target_pairs={{0,8},{8,16},{16,24},{24,32},{32,40},{40,48},{48,56},{56,64},{64,7... | collective-permute-start | bytes 3145736 | tf_op jit(solution)/shard_map/ppermute | solution.py:10
  4.8 15.0 %all_gather.6 = bf16[3,3,3,128,128]{3,4,2,1,0:T(8,128)(2,1)S(1)} all-gather(bf16[3,3,3,128,16]{3,4,2,1,0:T(8,128)(2,1)} %param.5), channel_id=1, replica_groups=mesh['tm'=32,'fsdp'=8] {'fsdp'}, dimensions={4}, use_global_device_ids=true | all-gather | bytes 995328 | tf_op jit(solution)/shard_map/all_gather | solution.py:41
  19.8 7.0 %collective-permute-done = bf16[2,64,32,128]{3,2,1,0:T(8,128)(2,1)S(1)} collective-permute-done((bf16[2,64,32,128]{3,2,1,0:T(8,128)(2,1)}, bf16[2,64,32,128]{3,2,1,0:T(8,128)(2,1)S(1)}, u32[]{:S(2)}, u32[]{:S(2)}) %collective-permute-start) | collective-permute-done | bytes 1048608 | tf_op jit(solution)/shard_map/ppermute | solution.py:10
  27.1 0.9 fusion.17
  28.0 3.4 %collective-permute-start.2 = (bf16[4,64,1,128]{3,2,1,0:T(2,128)(2,1)}, bf16[4,64,1,128]{3,2,1,0:T(2,128)(2,1)S(1)}, u32[]{:S(2)}, u32[]{:S(2)}) collective-permute-start(bf16[4,64,1,128]{3,2,1,0:T(2,128)(2,1)} %get-tuple-element.30), channel_id=1, source_target_pairs={{1,0},{2,1},{3,2},{4,3},{5,4},{6,5},{7,6},{9,8},{10,9},{11,10},{12... | collective-permute-start | bytes 196616 | tf_op jit(solution)/shard_map/ppermute | solution.py:23
  31.5 3.1 %collective-permute-start.1 = (bf16[4,64,1,128]{3,2,1,0:T(2,128)(2,1)}, bf16[4,64,1,128]{3,2,1,0:T(2,128)(2,1)S(1)}, u32[]{:S(2)}, u32[]{:S(2)}) collective-permute-start(bf16[4,64,1,128]{3,2,1,0:T(2,128)(2,1)} %get-tuple-element.29), channel_id=1, source_target_pairs={{0,1},{1,2},{2,3},{3,4},{4,5},{5,6},{6,7},{8,9},{9,10},{10,11},{11... | collective-permute-start | bytes 196616 | tf_op jit(solution)/shard_map/ppermute | solution.py:21
  34.6 0.8 fusion.18
  35.3 1.6 %copy.19 = bf16[3,1,1,128,128]{4,3,0,2,1:T(8,128)(2,1)} copy(bf16[3,1,1,128,128]{3,4,2,1,0:T(8,128)(2,1)} %get-tuple-element.39) | data formatting | bytes 196608
  37.0 0.8 copy.20
  38.4 1.0 copy.26
  39.4 1.6 %copy.27 = bf16[3,1,1,128,128]{4,3,0,2,1:T(8,128)(2,1)} copy(bf16[3,1,1,128,128]{3,4,2,1,0:T(8,128)(2,1)} %get-tuple-element.31) | data formatting | bytes 196608
  41.1 1.5 %fusion.7 = bf16[4,66,34,128]{3,2,1,0:T(8,128)(2,1)S(1)} fusion(bf16[4,64,1,128]{3,2,1,0:T(2,128)(2,1)S(1)} %collective-permute-done.2, bf16[4,64,32,128]{3,2,1,0:T(8,128)(2,1)S(1)} %constant_dynamic-update-slice_fusion, bf16[4,64,1,128]{3,2,1,0:T(2,128)(2,1)S(1)} %collective-permute-done.1), kind=kLoop, calls=%fused_computation.30 | loop fusion | flops 13787136 | bytes 4526080 | tf_op jit(solution)/shard_map/concatenate | solution.py:19
  42.6 6.9 %fusion.16 = (bf16[2,64,32,128]{3,2,1,0:T(8,128)(2,1)S(1)}, bf16[2,64,32,128]{3,2,1,0:T(8,128)(2,1)S(1)}, bf16[2,64,32,128]{3,2,1,0:T(8,128)(2,1)S(1)}, bf16[2,6...) fusion(bf16[4,66,34,128]{3,2,1,0:T(8,128)(2,1)S(1)} %fusion.7), kind=kLoop, calls=%fused_computation.59 | loop fusion | bytes 37748736 | tf_op jit(solution)/shard_map/slice | solution.py:54
  49.5 3.3 %pad_maximum_fusion.2 = (bf16[2,64,32,384]{3,2,1,0:T(8,128)(2,1)S(1)}, bf16[2,64,32,384]{3,2,1,0:T(8,128)(2,1)S(1)}) fusion(bf16[2,64,32,128]{3,2,1,0:T(8,128)(2,1)} %get-tuple-element.16, bf16[2,64,32,128]{3,2,1,0:T(8,128)(2,1)} %get-tuple-element.17, bf16[2,64,32,128]{3,2,1,0:T(8,128)(2,1)} %get-tuple-element.18, ...), kind=kLoop, calls=%fused_computation.19 | loop fusion | flops 18874368 | bytes 12582912 | tf_op jit(solution)/shard_map/concatenate | solution.py:52
  52.8 1.0 fusion.19
  53.9 1.1 convolution_add_fusion.7
  55.0 0.3 copy-done.2
  55.4 0.3 copy-done.3
  55.7 0.3 copy-done.4
  56.0 0.9 pad_maximum_fusion.4
  56.9 1.0 convolution_add_fusion.6
  57.8 2.1 %fusion.10 = (bf16[2,64,32,128]{3,2,1,0:T(8,128)(2,1)S(1)}, bf16[2,64,32,128]{3,2,1,0:T(8,128)(2,1)S(1)}, bf16[2,64,32,128]{3,2,1,0:T(8,128)(2,1)S(1)}, bf16[2,6...) fusion(bf16[4,64,32,128]{3,2,1,0:T(8,128)(2,1)S(1)} %constant_dynamic-update-slice_fusion, ...), kind=kLoop, calls=%fused_computation.44 | loop fusion | flops 8388608 | bytes 8650752 | tf_op jit(solution)/shard_map/concatenate | solution.py:19
  60.0 2.5 %fusion.1 = (bf16[2,64,32,384]{3,2,1,0:T(8,128)(2,1)S(1)}, bf16[2,64,32,384]{3,2,1,0:T(8,128)(2,1)S(1)}) fusion(bf16[4,64,1,128]{3,2,1,0:T(2,128)(2,1)S(1)} %collective-permute-done.2, bf16[4,64,32,128]{3,2,1,0:T(8,128)(2,1)S(1)} %constant_dynamic-update-slice_fusion, bf16[2,64,32,128]{3,2,1,0:T(8,128)(2,1)S(1)} %get-tuple-element.21, ...), kind=kLoop, calls=%fused_computation.16 | loop fusion | flops 25165824 | bytes 12713984 | tf_op jit(solution)/shard_map/concatenate | solution.py:52
  62.5 1.0 convolution_add_fusion.5
  63.7 0.3 copy-done.8
  64.0 0.4 pad_maximum_fusion.5
  64.5 1.0 convolution_add_fusion.4
  65.5 1.0 convolution_add_fusion.3
  66.5 1.0 convolution_add_fusion.2
  67.5 0.9 pad_maximum_fusion.7
  68.4 1.0 convolution_add_fusion.1
  69.5 1.1 multiply_convert_fusion
  70.6 0.3 convert.1
  70.9 1.0 fusion.15
  71.9 12.8 %all-to-all-start = ((bf16[1,64,32,128]{3,2,0,1:T(8,128)(2,1)}), bf16[1,64,32,128]{3,2,0,1:T(8,128)(2,1)S(1)}, u32[]{:S(2)}, u32[]{:S(2)}) async-start(bf16[1,64,32,128]{3,2,0,1:T(8,128)(2,1)} %fusion.15), calls=%async_computation | async-start | bytes 1048576 | tf_op jit(solution)/shard_map/all_to_all | solution.py:67
  84.8 12.7 %all_gather.7 = bf16[3,128,128]{1,2,0:T(8,128)(2,1)S(1)} all-gather(bf16[3,128,16]{1,2,0:T(8,128)(2,1)S(1)} %copy-done.12), channel_id=1, replica_groups=mesh['tm'=32,'fsdp'=8] {'fsdp'}, dimensions={2}, use_global_device_ids=true | all-gather | bytes 110592 | tf_op jit(solution)/shard_map/all_gather | solution.py:42
  97.4 4.7 %all-to-all-done = bf16[1,64,32,128]{3,2,0,1:T(8,128)(2,1)S(1)} async-done(((bf16[1,64,32,128]{3,2,0,1:T(8,128)(2,1)}), bf16[1,64,32,128]{3,2,0,1:T(8,128)(2,1)S(1)}, u32[]{:S(2)}, u32[]{:S(2)}) %all-to-all-start) | async-done | bytes 524320 | tf_op jit(solution)/shard_map/all_to_all | solution.py:67
  102.1 0.2 pad_slice_fusion.8
  102.4 0.3 convolution_bitcast_fusion
  102.7 0.3 convolution_bitcast_fusion.1
  103.0 0.3 convolution_add_fusion.10
  103.3 0.3 convolution_bitcast_fusion.2
  103.7 1.1 all_to_all.22
  104.9 8.5 %all-to-all-start.1 = ((f32[256,1,192]{2,1,0:T(1,128)}), f32[256,1,192]{2,1,0:T(1,128)S(1)}, u32[]{:S(2)}, u32[]{:S(2)}) async-start(f32[256,1,192]{2,1,0:T(1,128)} %all_to_all.22), calls=%async_computation.1 | async-start | bytes 524288 | tf_op jit(solution)/shard_map/all_to_all | solution.py:81
  113.4 0.3 convolution_add_fusion.9
  113.7 1.1 fusion.8
  114.8 13.9 %all-to-all-done.1 = f32[256,1,192]{2,1,0:T(1,128)S(1)} async-done(((f32[256,1,192]{2,1,0:T(1,128)}), f32[256,1,192]{2,1,0:T(1,128)S(1)}, u32[]{:S(2)}, u32[]{:S(2)}) %all-to-all-start.1) | async-done | bytes 196640 | tf_op jit(solution)/shard_map/all_to_all | solution.py:81
  128.7 0.9 reduce_sum.9
  (32 shorter events, 1.3 us)
Async XLA Ops:
  0.6 101.7 %copy-start = (bf16[32,2,32,128]{3,2,1,0:T(8,128)(2,1)S(1)}, bf16[32,2,32,128]{3,2,1,0:T(8,128)(2,1)}, u32[]{:S(2)}) copy-start(bf16[32,2,32,128]{3,2,1,0:T(8,128)(2,1)} %param.7) | copy-start | bytes 1572868
  0.6 26.3 %copy-start.5 = (bf16[2,64,32,128]{3,2,1,0:T(8,128)(2,1)S(1)}, bf16[2,64,32,128]{3,2,1,0:T(8,128)(2,1)}, u32[]{:S(2)}) copy-start(bf16[2,64,32,128]{3,2,1,0:T(8,128)(2,1)} %param.4) | copy-start | bytes 3145732
  0.7 26.2 %collective-permute-start = (bf16[2,64,32,128]{3,2,1,0:T(8,128)(2,1)}, bf16[2,64,32,128]{3,2,1,0:T(8,128)(2,1)S(1)}, u32[]{:S(2)}, u32[]{:S(2)}) collective-permute-start(bf16[2,64,32,128]{3,2,1,0:T(8,128)(2,1)} %param.4), channel_id=1, source_target_pairs={{0,8},{8,16},{16,24},{24,32},{32,40},{40,48},{48,56},{56,64},{64,7... | collective-permute-start | bytes 3145736 | tf_op jit(solution)/shard_map/ppermute | solution.py:10
  26.9 8.5 %copy-start.7 = (bf16[2,64,32,128]{3,2,1,0:T(8,128)(2,1)}, bf16[2,64,32,128]{3,2,1,0:T(8,128)(2,1)S(1)}, u32[]{:S(2)}) copy-start(bf16[2,64,32,128]{3,2,1,0:T(8,128)(2,1)S(1)} %collective-permute-done) | copy-start | bytes 3145732
  28.0 13.0 %collective-permute-start.2 = (bf16[4,64,1,128]{3,2,1,0:T(2,128)(2,1)}, bf16[4,64,1,128]{3,2,1,0:T(2,128)(2,1)S(1)}, u32[]{:S(2)}, u32[]{:S(2)}) collective-permute-start(bf16[4,64,1,128]{3,2,1,0:T(2,128)(2,1)} %get-tuple-element.30), channel_id=1, source_target_pairs={{1,0},{2,1},{3,2},{4,3},{5,4},{6,5},{7,6},{9,8},{10,9},{11,10},{12... | collective-permute-start | bytes 196616 | tf_op jit(solution)/shard_map/ppermute | solution.py:23
  31.5 9.6 %collective-permute-start.1 = (bf16[4,64,1,128]{3,2,1,0:T(2,128)(2,1)}, bf16[4,64,1,128]{3,2,1,0:T(2,128)(2,1)S(1)}, u32[]{:S(2)}, u32[]{:S(2)}) collective-permute-start(bf16[4,64,1,128]{3,2,1,0:T(2,128)(2,1)} %get-tuple-element.29), channel_id=1, source_target_pairs={{0,1},{1,2},{2,3},{3,4},{4,5},{5,6},{6,7},{8,9},{9,10},{10,11},{11... | collective-permute-start | bytes 196616 | tf_op jit(solution)/shard_map/ppermute | solution.py:21
  49.5 3.3 %copy-start.10 = (bf16[3,1,1,128,128]{4,3,0,2,1:T(8,128)(2,1)S(1)}, bf16[3,1,1,128,128]{4,3,0,2,1:T(8,128)(2,1)}, u32[]{:S(2)}) copy-start(bf16[3,1,1,128,128]{4,3,0,2,1:T(8,128)(2,1)} %copy.19) | copy-start | bytes 294916
  52.8 1.0 copy-start.9
  53.8 1.2 copy-start.1
  53.8 1.5 %copy-start.2 = (bf16[2,64,32,128]{3,2,1,0:T(8,128)(2,1)S(1)}, bf16[2,64,32,128]{3,2,1,0:T(8,128)(2,1)}, u32[]{:S(2)}) copy-start(bf16[2,64,32,128]{3,2,1,0:T(8,128)(2,1)} %get-tuple-element.10) | copy-start | bytes 3145732
  53.8 1.8 %copy-start.3 = (bf16[2,64,32,128]{3,2,1,0:T(8,128)(2,1)S(1)}, bf16[2,64,32,128]{3,2,1,0:T(8,128)(2,1)}, u32[]{:S(2)}) copy-start(bf16[2,64,32,128]{3,2,1,0:T(8,128)(2,1)} %get-tuple-element.11) | copy-start | bytes 3145732
  53.8 2.1 %copy-start.4 = (bf16[2,64,32,128]{3,2,1,0:T(8,128)(2,1)S(1)}, bf16[2,64,32,128]{3,2,1,0:T(8,128)(2,1)}, u32[]{:S(2)}) copy-start(bf16[2,64,32,128]{3,2,1,0:T(8,128)(2,1)} %get-tuple-element.12) | copy-start | bytes 3145732
  62.5 1.2 copy-start.6
  62.5 1.5 %copy-start.8 = (bf16[2,64,32,128]{3,2,1,0:T(8,128)(2,1)S(1)}, bf16[2,64,32,128]{3,2,1,0:T(8,128)(2,1)}, u32[]{:S(2)}) copy-start(bf16[2,64,32,128]{3,2,1,0:T(8,128)(2,1)} %copy-done.7) | copy-start | bytes 3145732
  68.4 1.0 copy-start.11
  70.6 14.1 %copy-start.12 = (bf16[3,128,16]{1,2,0:T(8,128)(2,1)S(1)}, bf16[3,128,16]{1,2,0:T(8,128)(2,1)}, u32[]{:S(2)}) copy-start(bf16[3,128,16]{1,2,0:T(8,128)(2,1)} %param.6) | copy-start | bytes 36868
  71.9 30.2 %all-to-all-start = ((bf16[1,64,32,128]{3,2,0,1:T(8,128)(2,1)}), bf16[1,64,32,128]{3,2,0,1:T(8,128)(2,1)S(1)}, u32[]{:S(2)}, u32[]{:S(2)}) async-start(bf16[1,64,32,128]{3,2,0,1:T(8,128)(2,1)} %fusion.15), calls=%async_computation | async-start | bytes 1048576 | tf_op jit(solution)/shard_map/all_to_all | solution.py:67
  104.9 23.8 %all-to-all-start.1 = ((f32[256,1,192]{2,1,0:T(1,128)}), f32[256,1,192]{2,1,0:T(1,128)S(1)}, u32[]{:S(2)}, u32[]{:S(2)}) async-start(f32[256,1,192]{2,1,0:T(1,128)} %all_to_all.22), calls=%async_computation.1 | async-start | bytes 524288 | tf_op jit(solution)/shard_map/all_to_all | solution.py:81
where the time goes:
time: 130 us
  starting transfers between devices  32 us (25%)
  blocking collectives  27.7 us (21%)
  waiting for transfers between devices  25.6 us (20%)
  local copies, waits for them, and re-layouts  17.5 us (13%)
  other arithmetic  13.8 us (11%)
  matrix products  11.9 us (9%)
    all_gather x1, blocking collectives, local(): lax.all_gather(conv_weight, 'fsdp', axis=4, tiled=True)  15 us
    all_to_all x1, waiting for transfers between devices, local(): lax.all_to_all(jnp.stack(grad_terms).reshape(parts, -1), ('tm', 'fsdp'),...  13.9 us
    all_to_all x1, starting transfers between devices, local(): lax.all_to_all(pool_pairs(hidden), 'tm', split_axis=1, concat_axis=0, til...  12.8 us
    all_gather x1, blocking collectives, local(): lax.all_gather(mix_weight, 'fsdp', axis=2, tiled=True)  12.7 us
    dot_general x9, matrix products, local(): accum = accum + jnp.dot(stacked, kernel, preferred_element_type=jnp.float32)  9.18 us
    all_to_all x1, starting transfers between devices, local(): lax.all_to_all(jnp.stack(grad_terms).reshape(parts, -1), ('tm', 'fsdp'),...  8.54 us
    concatenate x5, other arithmetic, local(): jnp.concatenate([padded[step:step + count_frames, row_tap:row_tap + heigh...  7.93 us
    unnamed x36, local copies, waits for them, and re-layouts  7.4 us
  transfers between devices with their start and end apart: 5, of which 3 were waited for; matrix products, arithmetic and copies ran while one was open for 6% of the time, Pallas kernels for 0%

commit v1 on v0

--- a/solution.py
+++ b/solution.py
@@ -64,7 +64,12 @@
             kernel = full_conv[:, row_tap, col_tap].reshape(3 * channels, channels)
             accum = accum + jnp.dot(stacked, kernel, preferred_element_type=jnp.float32)
     hidden = jax.nn.silu(accum).astype(jnp.bfloat16).reshape(count_frames, height, width, channels)
-    pooled = lax.all_to_all(pool_pairs(hidden), "tm", split_axis=1, concat_axis=0, tiled=True)
+    pooled = jnp.concatenate(
+        lax.all_to_all(
+            jnp.stack(jnp.split(pool_pairs(hidden), lax.axis_size("tm"), axis=1)), "tm", 0, 0
+        ),
+        axis=0,
+    )
     branch = pooled.astype(jnp.float32).reshape(-1, channels)
     flat_cot = cotangent.reshape(-1, channels)
     grad_terms = []

time: 130 us -> 149 us (1.15)
  local copies, waits for them, and re-layouts: 17.5 us -> 36.9 us
    unnamed x36 -> x67, local copies, waits for them, and re-layouts: 7.4 us -> 26.2 us
  transfers between devices with their start and end apart: 5 -> 5, of which waited for: 3 -> 3; matrix products, arithmetic and copies ran while one was open for 6% -> 5% of each run, Pallas kernels for 0% -> 0%
where the time goes in v1:
time: 149 us; the launch traced here: 148 us
  local copies, waits for them, and re-layouts  36.9 us (25%)
  starting transfers between devices  32 us (21%)
  blocking collectives  27.7 us (19%)
  waiting for transfers between devices  25.6 us (17%)
  other arithmetic  13 us (9%)
  matrix products  11.9 us (8%)
    unnamed x67, local copies, waits for them, and re-layouts  26.2 us
    all_gather x1, blocking collectives, local(): lax.all_gather(conv_weight, 'fsdp', axis=4, tiled=True)  15 us
    all_to_all x1, waiting for transfers between devices, local(): lax.all_to_all(jnp.stack(grad_terms).reshape(parts, -1), ('tm', 'fsdp'),...  13.9 us
    all_to_all x1, starting transfers between devices, local(): lax.all_to_all(jnp.stack(jnp.split(pool_pairs(hidden), lax.axis_size('tm'...  12.8 us
    all_gather x1, blocking collectives, local(): lax.all_gather(mix_weight, 'fsdp', axis=2, tiled=True)  12.7 us
    dot_general x9, matrix products, local(): accum = accum + jnp.dot(stacked, kernel, preferred_element_type=jnp.float32)  9.18 us
    all_to_all x1, starting transfers between devices, local(): lax.all_to_all(jnp.stack(grad_terms).reshape(parts, -1), ('tm', 'fsdp'),...  8.53 us
    concatenate x5, other arithmetic, local(): jnp.concatenate([padded[step:step + count_frames, row_tap:row_tap + heigh...  7.93 us
  transfers between devices with their start and end apart: 5, of which 3 were waited for; matrix products, arithmetic and copies ran while one was open for 5% of the time, Pallas kernels for 0%

profile of v1, /device:TPU:1, one launch (start us, length us, event | category | flops | bytes accessed | tf_op | source)
XLA Modules:
  0.0 148.1 jit_solution(18104271132035608237)
XLA Ops:
  0.7 4.1 %collective-permute-start = (bf16[2,64,32,128]{3,2,1,0:T(8,128)(2,1)}, bf16[2,64,32,128]{3,2,1,0:T(8,128)(2,1)S(1)}, u32[]{:S(2)}, u32[]{:S(2)}) collective-permute-start(bf16[2,64,32,128]{3,2,1,0:T(8,128)(2,1)} %param.4), channel_id=1, source_target_pairs={{0,8},{8,16},{16,24},{24,32},{32,40},{40,48},{48,56},{56,64},{64,7... | collective-permute-start | bytes 3145736 | tf_op jit(solution)/shard_map/ppermute | solution.py:10
  4.8 15.0 %all_gather.6 = bf16[3,3,3,128,128]{3,4,2,1,0:T(8,128)(2,1)S(1)} all-gather(bf16[3,3,3,128,16]{3,4,2,1,0:T(8,128)(2,1)} %param.5), channel_id=1, replica_groups=mesh['tm'=32,'fsdp'=8] {'fsdp'}, dimensions={4}, use_global_device_ids=true | all-gather | bytes 995328 | tf_op jit(solution)/shard_map/all_gather | solution.py:41
  19.8 7.0 %collective-permute-done = bf16[2,64,32,128]{3,2,1,0:T(8,128)(2,1)S(1)} collective-permute-done((bf16[2,64,32,128]{3,2,1,0:T(8,128)(2,1)}, bf16[2,64,32,128]{3,2,1,0:T(8,128)(2,1)S(1)}, u32[]{:S(2)}, u32[]{:S(2)}) %collective-permute-start) | collective-permute-done | bytes 1048608 | tf_op jit(solution)/shard_map/ppermute | solution.py:10
  27.1 0.9 fusion.19
  28.0 3.4 %collective-permute-start.2 = (bf16[4,64,1,128]{3,2,1,0:T(2,128)(2,1)}, bf16[4,64,1,128]{3,2,1,0:T(2,128)(2,1)S(1)}, u32[]{:S(2)}, u32[]{:S(2)}) collective-permute-start(bf16[4,64,1,128]{3,2,1,0:T(2,128)(2,1)} %get-tuple-element.30), channel_id=1, source_target_pairs={{1,0},{2,1},{3,2},{4,3},{5,4},{6,5},{7,6},{9,8},{10,9},{11,10},{12... | collective-permute-start | bytes 196616 | tf_op jit(solution)/shard_map/ppermute | solution.py:23
  31.5 3.1 %collective-permute-start.1 = (bf16[4,64,1,128]{3,2,1,0:T(2,128)(2,1)}, bf16[4,64,1,128]{3,2,1,0:T(2,128)(2,1)S(1)}, u32[]{:S(2)}, u32[]{:S(2)}) collective-permute-start(bf16[4,64,1,128]{3,2,1,0:T(2,128)(2,1)} %get-tuple-element.29), channel_id=1, source_target_pairs={{0,1},{1,2},{2,3},{3,4},{4,5},{5,6},{6,7},{8,9},{9,10},{10,11},{11... | collective-permute-start | bytes 196616 | tf_op jit(solution)/shard_map/ppermute | solution.py:21
  34.6 0.8 fusion.20
  35.3 1.6 %copy.81 = bf16[3,1,1,128,128]{4,3,0,2,1:T(8,128)(2,1)} copy(bf16[3,1,1,128,128]{3,4,2,1,0:T(8,128)(2,1)} %get-tuple-element.39) | data formatting | bytes 196608
  37.0 0.8 copy.82
  38.4 1.0 copy.88
  39.4 1.6 %copy.89 = bf16[3,1,1,128,128]{4,3,0,2,1:T(8,128)(2,1)} copy(bf16[3,1,1,128,128]{3,4,2,1,0:T(8,128)(2,1)} %get-tuple-element.31) | data formatting | bytes 196608
  41.1 1.5 %fusion.7 = bf16[4,66,34,128]{3,2,1,0:T(8,128)(2,1)S(1)} fusion(bf16[4,64,1,128]{3,2,1,0:T(2,128)(2,1)S(1)} %collective-permute-done.2, bf16[4,64,32,128]{3,2,1,0:T(8,128)(2,1)S(1)} %constant_dynamic-update-slice_fusion, bf16[4,64,1,128]{3,2,1,0:T(2,128)(2,1)S(1)} %collective-permute-done.1), kind=kLoop, calls=%fused_computation.30 | loop fusion | flops 13787136 | bytes 4526080 | tf_op jit(solution)/shard_map/concatenate | solution.py:19
  42.6 6.9 %fusion.18 = (bf16[2,64,32,128]{3,2,1,0:T(8,128)(2,1)S(1)}, bf16[2,64,32,128]{3,2,1,0:T(8,128)(2,1)S(1)}, bf16[2,64,32,128]{3,2,1,0:T(8,128)(2,1)S(1)}, bf16[2,6...) fusion(bf16[4,66,34,128]{3,2,1,0:T(8,128)(2,1)S(1)} %fusion.7), kind=kLoop, calls=%fused_computation.125 | loop fusion | bytes 37748736 | tf_op jit(solution)/shard_map/slice | solution.py:54
  49.5 3.3 %pad_maximum_fusion.2 = (bf16[2,64,32,384]{3,2,1,0:T(8,128)(2,1)S(1)}, bf16[2,64,32,384]{3,2,1,0:T(8,128)(2,1)S(1)}) fusion(bf16[2,64,32,128]{3,2,1,0:T(8,128)(2,1)} %get-tuple-element.16, bf16[2,64,32,128]{3,2,1,0:T(8,128)(2,1)} %get-tuple-element.17, bf16[2,64,32,128]{3,2,1,0:T(8,128)(2,1)} %get-tuple-element.18, ...), kind=kLoop, calls=%fused_computation.19 | loop fusion | flops 18874368 | bytes 12582912 | tf_op jit(solution)/shard_map/concatenate | solution.py:52
  52.8 1.0 fusion.21
  53.9 1.1 convolution_add_fusion.7
  56.0 0.9 pad_maximum_fusion.4
  56.9 1.0 convolution_add_fusion.6
  57.8 2.1 %fusion.10 = (bf16[2,64,32,128]{3,2,1,0:T(8,128)(2,1)S(1)}, bf16[2,64,32,128]{3,2,1,0:T(8,128)(2,1)S(1)}, bf16[2,64,32,128]{3,2,1,0:T(8,128)(2,1)S(1)}, bf16[2,6...) fusion(bf16[4,64,32,128]{3,2,1,0:T(8,128)(2,1)S(1)} %constant_dynamic-update-slice_fusion, ...), kind=kLoop, calls=%fused_computation.44 | loop fusion | flops 8388608 | bytes 8650752 | tf_op jit(solution)/shard_map/concatenate | solution.py:19
  60.0 2.5 %fusion.1 = (bf16[2,64,32,384]{3,2,1,0:T(8,128)(2,1)S(1)}, bf16[2,64,32,384]{3,2,1,0:T(8,128)(2,1)S(1)}) fusion(bf16[4,64,1,128]{3,2,1,0:T(2,128)(2,1)S(1)} %collective-permute-done.2, bf16[4,64,32,128]{3,2,1,0:T(8,128)(2,1)S(1)} %constant_dynamic-update-slice_fusion, bf16[2,64,32,128]{3,2,1,0:T(8,128)(2,1)S(1)} %get-tuple-element.21, ...), kind=kLoop, calls=%fused_computation.16 | loop fusion | flops 25165824 | bytes 12713984 | tf_op jit(solution)/shard_map/concatenate | solution.py:52
  62.5 1.0 convolution_add_fusion.5
  64.5 1.0 convolution_add_fusion.4
  65.5 1.0 convolution_add_fusion.3
  66.5 1.0 convolution_add_fusion.2
  67.5 0.9 pad_maximum_fusion.7
  68.4 1.0 convolution_add_fusion.1
  69.5 1.1 multiply_convert_fusion
  71.1 0.6 constant_dynamic-update-slice_fusion.33
  71.7 0.6 constant_dynamic-update-slice_fusion.32
  72.3 0.6 constant_dynamic-update-slice_fusion.31
  72.9 0.6 constant_dynamic-update-slice_fusion.30
  73.6 0.6 constant_dynamic-update-slice_fusion.29
  74.2 0.6 constant_dynamic-update-slice_fusion.28
  74.8 0.6 constant_dynamic-update-slice_fusion.27
  75.4 0.6 constant_dynamic-update-slice_fusion.26
  77.2 0.6 constant_dynamic-update-slice_fusion.23
  77.8 0.6 constant_dynamic-update-slice_fusion.22
  78.4 0.6 constant_dynamic-update-slice_fusion.21
  79.0 0.6 constant_dynamic-update-slice_fusion.20
  79.6 0.6 constant_dynamic-update-slice_fusion.19
  90.5 12.8 %all-to-all-start = ((bf16[32,1,2,32,128]{4,3,2,1,0:T(8,128)(2,1)}), bf16[32,1,2,32,128]{4,3,2,1,0:T(8,128)(2,1)S(1)}, u32[]{:S(2)}, u32[]{:S(2)}) async-start(bf16[32,1,2,32,128]{4,3,2,1,0:T(8,128)(2,1)} %constant_dynamic-update-slice_fusion.2), calls=%async_computation | async-start | bytes 1048576 | tf_op jit(solution)/shard_map/all_to_all | solution.py:68
  103.4 12.7 %all_gather.7 = bf16[3,128,128]{1,2,0:T(8,128)(2,1)S(1)} all-gather(bf16[3,128,16]{1,2,0:T(8,128)(2,1)S(1)} %copy-done.12), channel_id=1, replica_groups=mesh['tm'=32,'fsdp'=8] {'fsdp'}, dimensions={2}, use_global_device_ids=true | all-gather | bytes 110592 | tf_op jit(solution)/shard_map/all_gather | solution.py:42
  116.0 4.7 %all-to-all-done = bf16[32,1,2,32,128]{4,3,2,1,0:T(8,128)(2,1)S(1)} async-done(((bf16[32,1,2,32,128]{4,3,2,1,0:T(8,128)(2,1)}), bf16[32,1,2,32,128]{4,3,2,1,0:T(8,128)(2,1)S(1)}, u32[]{:S(2)}, u32[]{:S(2)}) %all-to-all-start) | async-done | bytes 524320 | tf_op jit(solution)/shard_map/all_to_all | solution.py:68
  122.3 1.1 all_to_all.12
  123.5 8.5 %all-to-all-start.1 = ((f32[256,1,192]{2,1,0:T(1,128)}), f32[256,1,192]{2,1,0:T(1,128)S(1)}, u32[]{:S(2)}, u32[]{:S(2)}) async-start(f32[256,1,192]{2,1,0:T(1,128)} %all_to_all.12), calls=%async_computation.1 | async-start | bytes 524288 | tf_op jit(solution)/shard_map/all_to_all | solution.py:86
  132.3 1.1 fusion.8
  133.4 13.9 %all-to-all-done.1 = f32[256,1,192]{2,1,0:T(1,128)S(1)} async-done(((f32[256,1,192]{2,1,0:T(1,128)}), f32[256,1,192]{2,1,0:T(1,128)S(1)}, u32[]{:S(2)}, u32[]{:S(2)}) %all-to-all-start.1) | async-done | bytes 196640 | tf_op jit(solution)/shard_map/all_to_all | solution.py:86
  147.3 0.9 reduce_sum.9
  (64 shorter events, 16.8 us)
Async XLA Ops:
  0.6 120.7 %copy-start = (bf16[32,2,32,128]{3,2,1,0:T(8,128)(2,1)S(1)}, bf16[32,2,32,128]{3,2,1,0:T(8,128)(2,1)}, u32[]{:S(2)}) copy-start(bf16[32,2,32,128]{3,2,1,0:T(8,128)(2,1)} %param.7) | copy-start | bytes 1572868
  0.6 26.3 %copy-start.5 = (bf16[2,64,32,128]{3,2,1,0:T(8,128)(2,1)S(1)}, bf16[2,64,32,128]{3,2,1,0:T(8,128)(2,1)}, u32[]{:S(2)}) copy-start(bf16[2,64,32,128]{3,2,1,0:T(8,128)(2,1)} %param.4) | copy-start | bytes 3145732
  0.7 26.2 %collective-permute-start = (bf16[2,64,32,128]{3,2,1,0:T(8,128)(2,1)}, bf16[2,64,32,128]{3,2,1,0:T(8,128)(2,1)S(1)}, u32[]{:S(2)}, u32[]{:S(2)}) collective-permute-start(bf16[2,64,32,128]{3,2,1,0:T(8,128)(2,1)} %param.4), channel_id=1, source_target_pairs={{0,8},{8,16},{16,24},{24,32},{32,40},{40,48},{48,56},{56,64},{64,7... | collective-permute-start | bytes 3145736 | tf_op jit(solution)/shard_map/ppermute | solution.py:10
  26.9 8.5 %copy-start.7 = (bf16[2,64,32,128]{3,2,1,0:T(8,128)(2,1)}, bf16[2,64,32,128]{3,2,1,0:T(8,128)(2,1)S(1)}, u32[]{:S(2)}) copy-start(bf16[2,64,32,128]{3,2,1,0:T(8,128)(2,1)S(1)} %collective-permute-done) | copy-start | bytes 3145732
  28.0 13.0 %collective-permute-start.2 = (bf16[4,64,1,128]{3,2,1,0:T(2,128)(2,1)}, bf16[4,64,1,128]{3,2,1,0:T(2,128)(2,1)S(1)}, u32[]{:S(2)}, u32[]{:S(2)}) collective-permute-start(bf16[4,64,1,128]{3,2,1,0:T(2,128)(2,1)} %get-tuple-element.30), channel_id=1, source_target_pairs={{1,0},{2,1},{3,2},{4,3},{5,4},{6,5},{7,6},{9,8},{10,9},{11,10},{12... | collective-permute-start | bytes 196616 | tf_op jit(solution)/shard_map/ppermute | solution.py:23
  31.5 9.6 %collective-permute-start.1 = (bf16[4,64,1,128]{3,2,1,0:T(2,128)(2,1)}, bf16[4,64,1,128]{3,2,1,0:T(2,128)(2,1)S(1)}, u32[]{:S(2)}, u32[]{:S(2)}) collective-permute-start(bf16[4,64,1,128]{3,2,1,0:T(2,128)(2,1)} %get-tuple-element.29), channel_id=1, source_target_pairs={{0,1},{1,2},{2,3},{3,4},{4,5},{5,6},{6,7},{8,9},{9,10},{10,11},{11... | collective-permute-start | bytes 196616 | tf_op jit(solution)/shard_map/ppermute | solution.py:21
  49.5 3.3 %copy-start.10 = (bf16[3,1,1,128,128]{4,3,0,2,1:T(8,128)(2,1)S(1)}, bf16[3,1,1,128,128]{4,3,0,2,1:T(8,128)(2,1)}, u32[]{:S(2)}) copy-start(bf16[3,1,1,128,128]{4,3,0,2,1:T(8,128)(2,1)} %copy.81) | copy-start | bytes 294916
  52.8 1.0 copy-start.9
  53.8 1.2 copy-start.1
  53.8 1.5 %copy-start.2 = (bf16[2,64,32,128]{3,2,1,0:T(8,128)(2,1)S(1)}, bf16[2,64,32,128]{3,2,1,0:T(8,128)(2,1)}, u32[]{:S(2)}) copy-start(bf16[2,64,32,128]{3,2,1,0:T(8,128)(2,1)} %get-tuple-element.10) | copy-start | bytes 3145732
  53.8 1.8 %copy-start.3 = (bf16[2,64,32,128]{3,2,1,0:T(8,128)(2,1)S(1)}, bf16[2,64,32,128]{3,2,1,0:T(8,128)(2,1)}, u32[]{:S(2)}) copy-start(bf16[2,64,32,128]{3,2,1,0:T(8,128)(2,1)} %get-tuple-element.11) | copy-start | bytes 3145732
  53.8 2.1 %copy-start.4 = (bf16[2,64,32,128]{3,2,1,0:T(8,128)(2,1)S(1)}, bf16[2,64,32,128]{3,2,1,0:T(8,128)(2,1)}, u32[]{:S(2)}) copy-start(bf16[2,64,32,128]{3,2,1,0:T(8,128)(2,1)} %get-tuple-element.12) | copy-start | bytes 3145732
  62.5 1.2 copy-start.6
  62.5 1.5 %copy-start.8 = (bf16[2,64,32,128]{3,2,1,0:T(8,128)(2,1)S(1)}, bf16[2,64,32,128]{3,2,1,0:T(8,128)(2,1)}, u32[]{:S(2)}) copy-start(bf16[2,64,32,128]{3,2,1,0:T(8,128)(2,1)} %copy-done.7) | copy-start | bytes 3145732
  68.4 1.0 copy-start.11
  70.9 32.5 %copy-start.12 = (bf16[3,128,16]{1,2,0:T(8,128)(2,1)S(1)}, bf16[3,128,16]{1,2,0:T(8,128)(2,1)}, u32[]{:S(2)}) copy-start(bf16[3,128,16]{1,2,0:T(8,128)(2,1)} %param.6) | copy-start | bytes 36868
  90.5 30.2 %all-to-all-start = ((bf16[32,1,2,32,128]{4,3,2,1,0:T(8,128)(2,1)}), bf16[32,1,2,32,128]{4,3,2,1,0:T(8,128)(2,1)S(1)}, u32[]{:S(2)}, u32[]{:S(2)}) async-start(bf16[32,1,2,32,128]{4,3,2,1,0:T(8,128)(2,1)} %constant_dynamic-update-slice_fusion.2), calls=%async_computation | async-start | bytes 1048576 | tf_op jit(solution)/shard_map/all_to_all | solution.py:68
  123.5 23.8 %all-to-all-start.1 = ((f32[256,1,192]{2,1,0:T(1,128)}), f32[256,1,192]{2,1,0:T(1,128)S(1)}, u32[]{:S(2)}, u32[]{:S(2)}) async-start(f32[256,1,192]{2,1,0:T(1,128)} %all_to_all.12), calls=%async_computation.1 | async-start | bytes 524288 | tf_op jit(solution)/shard_map/all_to_all | solution.py:86
